TPU v7x, 256 devices: a whole 4x4x8 slice. The times are simulated.
256 devices in a mesh: sub: 32 (over x, z_hi, core), coarse: 8 (over z_lo, y).
Axes of the slice: x: 4, y: 4, z: 8 (z_hi: 4, z_lo: 2; z = z_hi * 2 + z_lo), core: 2. Of those that a mesh axis runs over, the one named last changes fastest.
Arguments:
- residual_parts: bfloat16 [32, 8, 4, 256, 512], P('sub', 'coarse'), may hold values from -6 to 6
- face_slot: int32 [32, 8, 4], P('sub', 'coarse'), may hold values from 0 to 3, each once within a row
- face_order: int32 [32, 8, 4, 512], P('sub', 'coarse'), may hold values from 0 to 511, each once within a row
- face_scale: float32 [32, 8, 4], P('sub', 'coarse'), may hold values from 0 to 1, as said below
- vertex_unknowns: int32 [32, 8, 256], P('sub', 'coarse'), may hold values from 0 to 2047, all different within a row
- front_inverse: bfloat16 [32, 8, 2048, 2048], P('sub', 'coarse')
- coarse_basis: bfloat16 [32, 8, 2048, 256], P('sub', 'coarse'), may hold values from -0.125 to 0.125
- coarse_inverse: bfloat16 [32, 2048, 2048], P('sub', None, 'coarse'), as said below
- thermal_handoff: bfloat16 [32, 2048, 128], P('sub'), may hold values from -0.125 to 0.125
- chain_transfer: float32 [32, 128, 128], P('sub')
- coupling_in: bfloat16 [32, 128, 2048], P('sub', None, 'coarse'), may hold values from -0.5 to 0.5
Outputs:
- correction: bfloat16 [32, 8, 4, 256, 512], P('sub', 'coarse')
Inputs may be any that keep to these rules, and one draw needn't show every extreme that they name: `face_slot`: each row is a permutation of 0 to 3. `face_order`: each row is a permutation of 0 to 511. `vertex_unknowns`: the 256 entries of each subdomain are distinct. `face_scale`: the two weights of a shared face sum to one; a face on the outer boundary has weight one. `coarse_inverse`: each line's matrix is symmetric.
All inputs are finite; a program needn't handle non-finite values.
Results may differ from a plain program's by a relative error of at most 0.0059.
Values may be sent and summed in bfloat16 or wider, within the bound.
No kernel may reach another device: no remote copies, remote signals or barrier semaphores. Data moves between devices by JAX's collectives and lax.ppermute only.
A program may use at most 128 MiB of HBM per device.

v0:
```python
import jax
import jax.numpy as jnp
from jax import lax
from jax.sharding import PartitionSpec as P

HIGHEST = lax.Precision.HIGHEST


def with_halo(block, sides, width):
    for axis, dim in sides:
        count = lax.axis_size(axis)
        forward = [(i, i + 1) for i in range(count - 1)]
        backward = [(target, source) for source, target in forward]
        low = lax.ppermute(
            lax.slice_in_dim(block, block.shape[dim] - width, None, axis=dim), axis, forward
        )
        high = lax.ppermute(lax.slice_in_dim(block, 0, width, axis=dim), axis, backward)
        block = jnp.concatenate([low, block, high], axis=dim)
    return block


def carried_in(array, axis, combine, identity):
    peers, mine = (lax.axis_size(axis), lax.axis_index(axis))
    everything = jax.tree.map(lambda part: lax.all_gather(part, axis), array)
    start = jax.tree.map(
        lambda part, zero: jnp.broadcast_to(jnp.asarray(zero, part.dtype), part.shape),
        array,
        identity,
    )

    def step(k, before):
        reached = k < mine
        new = combine(before, jax.tree.map(lambda part: part[k], everything))
        return jax.tree.map(lambda a, b: jnp.where(reached, a, b), new, before)

    return lax.fori_loop(0, peers, step, start)


def build_tables(face_slot, face_order, table_type):
    face_count, block_size = face_order.shape
    slot_table = (
        face_slot[:, None] == lax.broadcasted_iota(jnp.int32, (face_count, face_count), 1)
    ).astype(table_type)
    order_table = (
        face_order[:, :, None]
        == lax.broadcasted_iota(jnp.int32, (face_count, block_size, block_size), 2)
    ).astype(table_type)
    return (slot_table, order_table)


def to_canonical(values, tables):
    slot_table, order_table = tables
    ordered = jnp.einsum(
        "snk,sjk->snj", values, order_table, preferred_element_type=jnp.float32, precision=HIGHEST
    ).astype(values.dtype)
    return jnp.einsum(
        "ds,snj->dnj", slot_table, ordered, preferred_element_type=jnp.float32, precision=HIGHEST
    ).astype(values.dtype)


def from_canonical(values, tables):
    slot_table, order_table = tables
    by_face = jnp.einsum(
        "ds,dnj->snj", slot_table, values, preferred_element_type=jnp.float32, precision=HIGHEST
    ).astype(values.dtype)
    return jnp.einsum(
        "snj,sjk->snk", by_face, order_table, preferred_element_type=jnp.float32, precision=HIGHEST
    ).astype(values.dtype)


def trade_faces(face_values):
    along_sub = with_halo(face_values[0:2], (("sub", 0),), 1)
    along_coarse = with_halo(face_values[2:4], (("coarse", 0),), 1)
    return jnp.stack([along_sub[0], along_sub[3], along_coarse[0], along_coarse[3]], 0)


def per_device(
    residual_parts,
    face_slot,
    face_order,
    face_scale,
    vertex_unknowns,
    front_inverse,
    coarse_basis,
    coarse_inverse,
    thermal_handoff,
    chain_transfer,
    coupling_in,
):
    own_parts = residual_parts[0, 0]
    own_slot = face_slot[0, 0]
    own_order = face_order[0, 0]
    own_scale = face_scale[0, 0][:, None, None]
    face_count, sample_count, block_size = own_parts.shape
    reduced_precision_tables = build_tables(own_slot, own_order, jnp.bfloat16)
    canon = to_canonical(own_parts, reduced_precision_tables)
    beside = trade_faces(canon)
    averaged = (own_scale * (canon.astype(jnp.float32) + beside.astype(jnp.float32))).astype(
        jnp.bfloat16
    )
    local_residual = from_canonical(averaged, reduced_precision_tables)
    own_primal = vertex_unknowns[0, 0]
    positions = lax.broadcasted_iota(jnp.int32, (own_primal.shape[0], face_count * block_size), 1)
    hits = jnp.sum((own_primal[:, None] == positions).astype(jnp.int32), axis=0)
    dual_mask = (1 - hits).astype(jnp.bfloat16).reshape(face_count, 1, block_size)
    inverse_blocks = front_inverse[0, 0].reshape(face_count, block_size, face_count, block_size)
    dual_part = (
        jnp.einsum(
            "gnj,gjfk->fnk",
            local_residual * dual_mask,
            inverse_blocks,
            preferred_element_type=jnp.float32,
        )
        * dual_mask
    )
    basis_blocks = coarse_basis[0, 0].reshape(face_count, block_size, -1)
    coarse_residual = jnp.einsum(
        "gnj,gjc->nc", local_residual, basis_blocks, preferred_element_type=jnp.float32
    ).astype(jnp.bfloat16)
    primal_count = coarse_residual.shape[1]
    line_block = coarse_inverse[0]
    line_outflow = thermal_handoff[0]
    channel_count = line_outflow.shape[1]
    line_base = lax.dot_general(
        line_block,
        lax.all_gather(coarse_residual, "coarse", axis=1, tiled=True),
        (((0,), (1,)), ((), ())),
        preferred_element_type=jnp.float32,
    )
    own_rows = lax.dynamic_slice_in_dim(
        line_outflow, lax.axis_index("coarse") * primal_count, primal_count, 0
    )
    inflow = lax.psum(
        jnp.dot(coarse_residual, own_rows, preferred_element_type=jnp.float32), "coarse"
    )
    transfer = chain_transfer[0]

    def compose(earlier, later):
        joined_map = jnp.dot(earlier[0], later[0], precision=HIGHEST)
        joined_state = jnp.dot(earlier[1], later[0], precision=HIGHEST) + later[1]
        return (joined_map, joined_state)

    identity = (jnp.eye(channel_count, dtype=jnp.float32), jnp.zeros_like(inflow))
    upstream_map, carried = carried_in((transfer, inflow), "sub", compose, identity)
    carried_term = lax.dot_general(
        coupling_in[0].astype(jnp.float32), carried, (((0,), (1,)), ((), ())), precision=HIGHEST
    )
    global_coarse_answer = (line_base + carried_term).astype(jnp.bfloat16)
    subregion_iterate = dual_part + jnp.einsum(
        "cn,gjc->gnj", global_coarse_answer, basis_blocks, preferred_element_type=jnp.float32
    )
    exact_tables = build_tables(own_slot, own_order, jnp.float32)
    weighted = (own_scale * to_canonical(subregion_iterate, exact_tables)).astype(jnp.bfloat16)
    beside_again = trade_faces(weighted)
    summed = (weighted.astype(jnp.float32) + beside_again.astype(jnp.float32)).astype(jnp.bfloat16)
    return from_canonical(summed, reduced_precision_tables)[None, None]


def solution(mesh):
    placed = (
        P("sub", "coarse", None, None, None),
        P("sub", "coarse", None),
        P("sub", "coarse", None, None),
        P("sub", "coarse", None),
        P("sub", "coarse", None),
        P("sub", "coarse", None, None),
        P("sub", "coarse", None, None),
        P("sub", None, "coarse"),
        P("sub", None, None),
        P("sub", None, None),
        P("sub", None, "coarse"),
    )
    return jax.shard_map(
        per_device,
        mesh=mesh,
        in_specs=placed,
        out_specs=P("sub", "coarse", None, None, None),
        check_vma=False,
    )
```

profile of v0, /device:TPU:26, one launch (start us, length us, event | category | flops | bytes accessed | tf_op | source)
XLA Modules:
  0.0 419.8 jit_solution(5209459540740825076)
XLA Ops:
  6.5 2.4 fusion.30
  11.1 2.3 fusion.70
  13.4 1.9 collective-permute-start
  15.4 7.6 %collective-permute-start.1 = (bf16[1,256,512]{2,0,1:T(2,128)(2,1)}, bf16[1,256,512]{2,0,1:T(2,128)(2,1)}, u32[]{:S(2)}, u32[]{:S(2)}) collective-permute-start(bf16[1,256,512]{2,0,1:T(2,128)(2,1)} %get-tuple-element.150), channel_id=1, source_target_pairs={{8,0},{16,8},{24,16},{32,24},{40,32},{48,40},{56,48},{64,56},{72,6... | collective-permute-start | bytes 786440 | tf_op jit(solution)/shard_map/ppermute | solution.py:17
  23.0 2.6 collective-permute-start.2
  25.6 3.3 collective-permute-start.3
  28.8 5.6 %collective-permute-done = bf16[1,256,512]{2,0,1:T(2,128)(2,1)} collective-permute-done((bf16[1,256,512]{2,0,1:T(2,128)(2,1)}, bf16[1,256,512]{2,0,1:T(2,128)(2,1)}, u32[]{:S(2)}, u32[]{:S(2)}) %collective-permute-start) | collective-permute-done | bytes 262176 | tf_op jit(solution)/shard_map/ppermute | solution.py:14
  34.5 1.2 collective-permute-done.1
  35.6 6.2 %collective-permute-done.2 = bf16[1,256,512]{2,0,1:T(2,128)(2,1)} collective-permute-done((bf16[1,256,512]{2,0,1:T(2,128)(2,1)S(1)}, bf16[1,256,512]{2,0,1:T(2,128)(2,1)}, u32[]{:S(2)}, u32[]{:S(2)}) %collective-permute-start.2) | collective-permute-done | bytes 262176 | tf_op jit(solution)/shard_map/ppermute | solution.py:14
  41.8 5.4 %collective-permute-done.3 = bf16[1,256,512]{2,0,1:T(2,128)(2,1)} collective-permute-done((bf16[1,256,512]{2,0,1:T(2,128)(2,1)S(1)}, bf16[1,256,512]{2,0,1:T(2,128)(2,1)}, u32[]{:S(2)}, u32[]{:S(2)}) %collective-permute-start.3) | collective-permute-done | bytes 262176 | tf_op jit(solution)/shard_map/ppermute | solution.py:17
  47.2 4.5 %convolution_convert_fusion.1 = bf16[4,256,512]{2,0,1:T(4,128)(2,1)S(1)} fusion(bf16[4,256,512]{2,0,1:T(4,128)(2,1)S(1)} %convolution_convert_fusion.2, bf16[1,256,512]{2,0,1:T(2,128)(2,1)} %collective-permute-done.3, bf16[1,256,512]{2,0,1:T(2,128)(2,1)} %collective-permute-done.2, bf16[1,256,512]{2,0,1:T(2,128)(2,1)} %collective-permute-done.1, ...), kind=kOutput, calls=%fused_computation.36 | convolution fusion | flops 11010064 | bytes 3145760 | tf_op jit(solution)/shard_map/ds,dnj->snj/dot_general | solution.py:63
  51.7 1.4 fusion.27
  54.5 1.7 convolution_bitcast_fusion.2
  57.9 75.5 %all-reduce.2.cloned.1.call-done = f32[1,256,128]{2,1,0:T(8,128)} async-done(((f32[1,256,128]{2,1,0:T(8,128)}), f32[1,256,128]{2,1,0:T(8,128)}) %all-reduce.2.cloned.1.call-update) | async-done | bytes 131088 | tf_op jit(solution)/shard_map/psum | solution.py:133
  133.9 14.5 %reshape_squeeze.6 = bf16[4,512,4,512]{3,2,1,0:T(4,128)(2,1)} reshape(bf16[1,1,2048,2048]{3,2,1,0:T(8,128)(2,1)} %param.18) | data formatting | bytes 16777216 | tf_op jit(solution)/shard_map/reshape;squeeze | solution.py:106
  148.4 6.5 %fusion.9 = f32[256,4,512,1]{2,0,3,1:T(8,128)S(1)} fusion(bf16[4,512,4,512]{3,2,1,0:T(4,128)(2,1)} %reshape_squeeze.6, bf16[4,256,512]{2,1,0:T(8,128)(2,1)} %copy-done.2, bf16[4,512]{1,0:T(4,128)(2,1)S(1)} %convert_element_type.89), kind=kOutput, calls=%fused_computation.11 | convolution fusion | flops 2149580800 | bytes 11538432 | tf_op jit(solution)/shard_map/gnj,gjfk->fnk/dot_general | solution.py:108
  155.0 22.1 %all-gather.4.cloned.1.call-done = bf16[256,2048]{1,0:T(8,128)(2,1)} async-done(((bf16[256,256]{1,0:T(8,128)(2,1)}), bf16[256,2048]{1,0:T(8,128)(2,1)}) %all-gather.4.cloned.1.call-update) | async-done | bytes 1048592 | tf_op jit(solution)/shard_map/all_gather | solution.py:126
  177.1 2.7 fusion.48
  179.8 54.5 %all-gather.6.cloned.1.call-done = f32[32,128,128]{2,1,0:T(8,128)} async-done(((f32[1,128,128]{2,1,0:T(8,128)}), f32[32,128,128]{2,1,0:T(8,128)}) %all-gather.6.cloned.1.call-update) | async-done | bytes 2097168 | tf_op jit(solution)/shard_map/all_gather | solution.py:24
  234.3 61.3 %all-gather.8.cloned.1.call-done = f32[32,256,128]{2,1,0:T(8,128)} async-done(((f32[1,256,128]{2,1,0:T(8,128)}), f32[32,256,128]{2,1,0:T(8,128)}) %all-gather.8.cloned.1.call-update) | async-done | bytes 4194320 | tf_op jit(solution)/shard_map/all_gather | solution.py:24
  295.6 71.3 %while.14 = (s32[]{:T(128)}, f32[256,128]{0,1:T(8,128)S(1)}, s32[]{:T(128)}, f32[32,128,128]{2,1,0:T(8,128)}, f32[32,256,128]{2,1,0:T(8,128)}, /*index=5*/s32[]{:T(128)}, s32[]{:T(128)}) while((s32[]{:T(128)}, f32[256,128]{0,1:T(8,128)S(1)}, s32[]{:T(128)}, f32[32,128,128]{2,1,0:T(8,128)}, f32[32,256,128]{2,1,0:T(8,128)}, ...), condition=%wide.region_3.4_spmd.clone, body=%wide.region_2.3_spmd.clone.sunk | while | flops 50462724 | bytes 1378403 | solution.py:36
  298.9 1.2 fusion.85
  303.3 1.2 fusion.85
  307.8 1.2 fusion.85
  312.2 1.2 fusion.85
  321.2 1.2 fusion.85
  325.6 1.2 fusion.85
  330.1 1.2 fusion.85
  334.5 1.2 fusion.85
  339.0 1.2 fusion.85
  347.9 1.2 fusion.85
  352.3 1.2 fusion.85
  356.8 1.2 fusion.85
  361.2 1.2 fusion.85
  365.7 1.2 fusion.85
  366.9 1.3 fusion.33
  368.7 2.8 fusion.12
  371.5 3.3 multiply_convert_fusion
  374.8 1.6 fusion.69
  376.4 2.2 collective-permute-start.4
  378.6 6.4 %collective-permute-start.5 = (bf16[1,256,512]{2,0,1:T(2,128)(2,1)S(1)}, bf16[1,256,512]{2,0,1:T(2,128)(2,1)S(1)}, u32[]{:S(2)}, u32[]{:S(2)}) collective-permute-start(bf16[1,256,512]{2,0,1:T(2,128)(2,1)S(1)} %get-tuple-element.146), channel_id=1, source_target_pairs={{8,0},{16,8},{24,16},{32,24},{40,32},{48,40},{56,48},{64,56},{72,6... | collective-permute-start | bytes 786440 | tf_op jit(solution)/shard_map/ppermute | solution.py:17
  385.0 2.1 collective-permute-start.6
  387.1 3.7 collective-permute-start.7
  390.9 5.8 %collective-permute-done.4 = bf16[1,256,512]{2,0,1:T(2,128)(2,1)S(1)} collective-permute-done((bf16[1,256,512]{2,0,1:T(2,128)(2,1)S(1)}, bf16[1,256,512]{2,0,1:T(2,128)(2,1)S(1)}, u32[]{:S(2)}, u32[]{:S(2)}) %collective-permute-start.4) | collective-permute-done | bytes 262176 | tf_op jit(solution)/shard_map/ppermute | solution.py:14
  397.1 5.4 %collective-permute-done.6 = bf16[1,256,512]{2,0,1:T(2,128)(2,1)S(1)} collective-permute-done((bf16[1,256,512]{2,0,1:T(2,128)(2,1)S(1)}, bf16[1,256,512]{2,0,1:T(2,128)(2,1)S(1)}, u32[]{:S(2)}, u32[]{:S(2)}) %collective-permute-start.6) | collective-permute-done | bytes 262176 | tf_op jit(solution)/shard_map/ppermute | solution.py:14
  402.4 5.8 %collective-permute-done.7 = bf16[1,256,512]{2,0,1:T(2,128)(2,1)S(1)} collective-permute-done((bf16[1,256,512]{2,0,1:T(2,128)(2,1)S(1)}, bf16[1,256,512]{2,0,1:T(2,128)(2,1)S(1)}, u32[]{:S(2)}, u32[]{:S(2)}) %collective-permute-start.7) | collective-permute-done | bytes 262176 | tf_op jit(solution)/shard_map/ppermute | solution.py:17
  408.2 2.9 convolution_convert_fusion
  411.1 2.2 fusion.29
  (150 shorter events, 59.9 us)
Async XLA Ops:
  6.5 46.5 %copy-start = (bf16[1,1,2048,256]{3,2,1,0:T(8,128)(2,1)S(1)}, bf16[1,1,2048,256]{3,2,1,0:T(8,128)(2,1)}, u32[]{:S(2)}) copy-start(bf16[1,1,2048,256]{3,2,1,0:T(8,128)(2,1)} %param.19) | copy-start | bytes 3145732
  6.5 126.9 %all-reduce.2.cloned.1.call-start = ((), (), s32[]{:S(2)}) async-start(), calls=%async_computation.2 | async-start | bytes 262144 | tf_op jit(solution)/shard_map/psum | solution.py:133
  6.5 3.5 copy-start.4
  11.1 36.1 %copy-start.7 = (f32[1,1,4]{2,1,0:T(1,128)S(1)}, f32[1,1,4]{2,1,0:T(1,128)}, u32[]{:S(2)}) copy-start(f32[1,1,4]{2,1,0:T(1,128)} %param.16) | copy-start | bytes 52
  13.4 21.0 %collective-permute-start = (bf16[1,256,512]{2,0,1:T(2,128)(2,1)}, bf16[1,256,512]{2,0,1:T(2,128)(2,1)}, u32[]{:S(2)}, u32[]{:S(2)}) collective-permute-start(bf16[1,256,512]{2,0,1:T(2,128)(2,1)} %get-tuple-element.147), channel_id=1, source_target_pairs={{0,8},{8,16},{16,24},{24,32},{32,40},{40,48},{48,56},{56,64},{64,7... | collective-permute-start | bytes 786440 | tf_op jit(solution)/shard_map/ppermute | solution.py:14
  15.4 20.3 %collective-permute-start.1 = (bf16[1,256,512]{2,0,1:T(2,128)(2,1)}, bf16[1,256,512]{2,0,1:T(2,128)(2,1)}, u32[]{:S(2)}, u32[]{:S(2)}) collective-permute-start(bf16[1,256,512]{2,0,1:T(2,128)(2,1)} %get-tuple-element.150), channel_id=1, source_target_pairs={{8,0},{16,8},{24,16},{32,24},{40,32},{48,40},{56,48},{64,56},{72,6... | collective-permute-start | bytes 786440 | tf_op jit(solution)/shard_map/ppermute | solution.py:17
  23.0 18.8 %collective-permute-start.2 = (bf16[1,256,512]{2,0,1:T(2,128)(2,1)S(1)}, bf16[1,256,512]{2,0,1:T(2,128)(2,1)}, u32[]{:S(2)}, u32[]{:S(2)}) collective-permute-start(bf16[1,256,512]{2,0,1:T(2,128)(2,1)S(1)} %get-tuple-element.149), channel_id=1, source_target_pairs={{0,1},{1,2},{2,3},{3,4},{4,5},{5,6},{6,7},{8,9},{9,10},{10,11},{11... | collective-permute-start | bytes 786440 | tf_op jit(solution)/shard_map/ppermute | solution.py:14
  25.6 21.6 %collective-permute-start.3 = (bf16[1,256,512]{2,0,1:T(2,128)(2,1)S(1)}, bf16[1,256,512]{2,0,1:T(2,128)(2,1)}, u32[]{:S(2)}, u32[]{:S(2)}) collective-permute-start(bf16[1,256,512]{2,0,1:T(2,128)(2,1)S(1)} %get-tuple-element.148), channel_id=1, source_target_pairs={{1,0},{2,1},{3,2},{4,3},{5,4},{6,5},{7,6},{9,8},{10,9},{11,10},{12... | collective-permute-start | bytes 786440 | tf_op jit(solution)/shard_map/ppermute | solution.py:17
  47.2 4.5 %copy-start.3 = (s32[1,1,4,512]{3,2,1,0:T(4,128)S(1)}, s32[1,1,4,512]{3,2,1,0:T(4,128)}, u32[]{:S(2)}) copy-start(s32[1,1,4,512]{3,2,1,0:T(4,128)} %param.15) | copy-start | bytes 24580
  53.1 1.0 copy-start.2
  53.1 80.5 %copy-start.6 = (s32[1,1,256]{2,1,0:T(1,128)S(1)}, s32[1,1,256]{2,1,0:T(1,128)}, u32[]{:S(2)}) copy-start(s32[1,1,256]{2,1,0:T(1,128)} %param.17) | copy-start | bytes 3076
  54.5 1.8 copy-start.1
  56.2 120.8 %all-gather.4.cloned.1.call-start = ((), (), s32[]{:S(2)}) async-start(), calls=%async_computation | async-start | bytes 1179648 | tf_op jit(solution)/shard_map/all_gather | solution.py:126
  57.0 177.3 %all-gather.6.cloned.1.call-start = ((), (), s32[]{:S(2)}) async-start(), calls=%async_computation.1 | async-start | bytes 2162688 | tf_op jit(solution)/shard_map/all_gather | solution.py:24
  57.7 237.9 %all-gather.8.cloned.1.call-start = ((), (), s32[]{:S(2)}) async-start(), calls=%async_computation.3 | async-start | bytes 4325376 | tf_op jit(solution)/shard_map/all_gather | solution.py:24
  368.7 2.8 copy-start.5
  368.7 2.8 copy-start.8
  376.4 20.3 %collective-permute-start.4 = (bf16[1,256,512]{2,0,1:T(2,128)(2,1)S(1)}, bf16[1,256,512]{2,0,1:T(2,128)(2,1)S(1)}, u32[]{:S(2)}, u32[]{:S(2)}) collective-permute-start(bf16[1,256,512]{2,0,1:T(2,128)(2,1)S(1)} %get-tuple-element.143), channel_id=1, source_target_pairs={{0,8},{8,16},{16,24},{24,32},{32,40},{40,48},{48,56},{56,64},{64,7... | collective-permute-start | bytes 786440 | tf_op jit(solution)/shard_map/ppermute | solution.py:14
  378.6 18.5 %collective-permute-start.5 = (bf16[1,256,512]{2,0,1:T(2,128)(2,1)S(1)}, bf16[1,256,512]{2,0,1:T(2,128)(2,1)S(1)}, u32[]{:S(2)}, u32[]{:S(2)}) collective-permute-start(bf16[1,256,512]{2,0,1:T(2,128)(2,1)S(1)} %get-tuple-element.146), channel_id=1, source_target_pairs={{8,0},{16,8},{24,16},{32,24},{40,32},{48,40},{56,48},{64,56},{72,6... | collective-permute-start | bytes 786440 | tf_op jit(solution)/shard_map/ppermute | solution.py:17
  385.0 17.5 %collective-permute-start.6 = (bf16[1,256,512]{2,0,1:T(2,128)(2,1)S(1)}, bf16[1,256,512]{2,0,1:T(2,128)(2,1)S(1)}, u32[]{:S(2)}, u32[]{:S(2)}) collective-permute-start(bf16[1,256,512]{2,0,1:T(2,128)(2,1)S(1)} %get-tuple-element.145), channel_id=1, source_target_pairs={{0,1},{1,2},{2,3},{3,4},{4,5},{5,6},{6,7},{8,9},{9,10},{10,11},{11... | collective-permute-start | bytes 786440 | tf_op jit(solution)/shard_map/ppermute | solution.py:14
  387.1 21.1 %collective-permute-start.7 = (bf16[1,256,512]{2,0,1:T(2,128)(2,1)S(1)}, bf16[1,256,512]{2,0,1:T(2,128)(2,1)S(1)}, u32[]{:S(2)}, u32[]{:S(2)}) collective-permute-start(bf16[1,256,512]{2,0,1:T(2,128)(2,1)S(1)} %get-tuple-element.144), channel_id=1, source_target_pairs={{1,0},{2,1},{3,2},{4,3},{5,4},{6,5},{7,6},{9,8},{10,9},{11,10},{12... | collective-permute-start | bytes 786440 | tf_op jit(solution)/shard_map/ppermute | solution.py:17
Sparse Core Ops, SparseCore 0:
  56.3 77.0 all-reduce.1
  135.3 41.7 all-gather.3
  180.0 54.2 all-gather.5
  237.0 58.5 all-gather.7
where the time goes:
time: 423 us; the launch traced here: 420 us
  waiting for transfers between devices  251 us (59%)
  matrix products  70.6 us (17%)
  local copies, waits for them, and re-layouts  53.2 us (13%)
  starting transfers between devices  30.1 us (7%)
  between operations  13.4 us (3%)
    all_gather x2, waiting for transfers between devices, carried_in(): everything = jax.tree.map(lambda part: lax.all_gather(part, axis), array)  116 us
    psum x1, waiting for transfers between devices, per_device(): lax.psum(jnp.dot(coarse_residual, own_rows, preferred_element_type=jnp.fl...  75.5 us
    dot_general x32, matrix products, compose(): joined_state = jnp.dot(earlier[1], later[0], precision=HIGHEST) + later[1]  37 us
    dynamic_slice x64, local copies, waits for them, and re-layouts, step(): new = combine(before, jax.tree.map(lambda part: part[k], everything))  32.4 us
    ppermute x4, waiting for transfers between devices, with_halo(): lax.ppermute(lax.slice_in_dim(block, block.shape[dim] - width, None, axis...  23 us
    all_gather x1, waiting for transfers between devices, per_device(): lax.all_gather(coarse_residual, 'coarse', axis=1, tiled=True)  22.1 us
    ppermute x4, starting transfers between devices, with_halo(): lax.ppermute(lax.slice_in_dim(block, 0, width, axis=dim), axis, backward)  21 us
    another operation x1, local copies, waits for them, and re-layouts, per_device(): front_inverse[0, 0].reshape(face_count, block_size, face_count, block_size)  14.5 us
  transfers between devices with their start and end apart: 12, of which 12 were waited for; matrix products, arithmetic and copies ran while one was open for 6% of the time, Pallas kernels for 0%

commit v1 on v0

--- a/solution.py
+++ b/solution.py
@@ -4,6 +4,11 @@
 from jax.sharding import PartitionSpec as P
 
 HIGHEST = lax.Precision.HIGHEST
+
+
+def gather_and_add(x, mesh_axis):
+    parts = lax.all_gather(x, mesh_axis)
+    return jnp.sum(parts, axis=0)
 
 
 def with_halo(block, sides, width):
@@ -130,7 +135,7 @@
     own_rows = lax.dynamic_slice_in_dim(
         line_outflow, lax.axis_index("coarse") * primal_count, primal_count, 0
     )
-    inflow = lax.psum(
+    inflow = gather_and_add(
         jnp.dot(coarse_residual, own_rows, preferred_element_type=jnp.float32), "coarse"
     )
     transfer = chain_transfer[0]

time: 423 us -> 385 us (0.910)
  waiting for transfers between devices: 251 us -> 210 us
    psum x1 -> x0, waiting for transfers between devices: 75.5 us -> none  [per_device(): lax.psum(jnp.dot(coarse_residual, own_rows, preferred_element_type=jnp.fl...]
    all_gather x0 -> x1, waiting for transfers between devices: none -> 38.6 us  [gather_and_add(): parts = lax.all_gather(x, mesh_axis)]
  transfers between devices with their start and end apart: 12 -> 12, of which waited for: 12 -> 12; matrix products, arithmetic and copies ran while one was open for 6% -> 7% of each run, Pallas kernels for 0% -> 0%
where the time goes in v1:
time: 385 us; the launch traced here: 382 us
  waiting for transfers between devices  210 us (55%)
  matrix products  70.7 us (18%)
  local copies, waits for them, and re-layouts  53.2 us (14%)
  starting transfers between devices  30.1 us (8%)
  between operations  13.4 us (3%)
    all_gather x2, waiting for transfers between devices, carried_in(): everything = jax.tree.map(lambda part: lax.all_gather(part, axis), array)  115 us
    all_gather x1, waiting for transfers between devices, gather_and_add(): parts = lax.all_gather(x, mesh_axis)  38.6 us
    dot_general x32, matrix products, compose(): joined_state = jnp.dot(earlier[1], later[0], precision=HIGHEST) + later[1]  37 us
    dynamic_slice x64, local copies, waits for them, and re-layouts, step(): new = combine(before, jax.tree.map(lambda part: part[k], everything))  32.4 us
    ppermute x4, waiting for transfers between devices, with_halo(): lax.ppermute(lax.slice_in_dim(block, block.shape[dim] - width, None, axis...  23 us
    ppermute x4, starting transfers between devices, with_halo(): lax.ppermute(lax.slice_in_dim(block, 0, width, axis=dim), axis, backward)  21 us
    all_gather x1, waiting for transfers between devices, per_device(): lax.all_gather(coarse_residual, 'coarse', axis=1, tiled=True)  19.6 us
    another operation x1, local copies, waits for them, and re-layouts, per_device(): front_inverse[0, 0].reshape(face_count, block_size, face_count, block_size)  14.5 us
  transfers between devices with their start and end apart: 12, of which 12 were waited for; matrix products, arithmetic and copies ran while one was open for 7% of the time, Pallas kernels for 0%

profile of v1, /device:TPU:26, one launch (start us, length us, event | category | flops | bytes accessed | tf_op | source)
XLA Modules:
  0.0 381.7 jit_solution(1335559288873125457)
XLA Ops:
  6.5 2.4 fusion.30
  11.1 2.3 fusion.71
  13.4 1.9 collective-permute-start
  15.4 7.6 %collective-permute-start.1 = (bf16[1,256,512]{2,0,1:T(2,128)(2,1)}, bf16[1,256,512]{2,0,1:T(2,128)(2,1)}, u32[]{:S(2)}, u32[]{:S(2)}) collective-permute-start(bf16[1,256,512]{2,0,1:T(2,128)(2,1)} %get-tuple-element.150), channel_id=1, source_target_pairs={{8,0},{16,8},{24,16},{32,24},{40,32},{48,40},{56,48},{64,56},{72,6... | collective-permute-start | bytes 786440 | tf_op jit(solution)/shard_map/ppermute | solution.py:22
  23.0 2.6 collective-permute-start.2
  25.6 3.3 collective-permute-start.3
  28.8 5.6 %collective-permute-done = bf16[1,256,512]{2,0,1:T(2,128)(2,1)} collective-permute-done((bf16[1,256,512]{2,0,1:T(2,128)(2,1)}, bf16[1,256,512]{2,0,1:T(2,128)(2,1)}, u32[]{:S(2)}, u32[]{:S(2)}) %collective-permute-start) | collective-permute-done | bytes 262176 | tf_op jit(solution)/shard_map/ppermute | solution.py:19
  34.5 1.2 collective-permute-done.1
  35.6 6.2 %collective-permute-done.2 = bf16[1,256,512]{2,0,1:T(2,128)(2,1)} collective-permute-done((bf16[1,256,512]{2,0,1:T(2,128)(2,1)S(1)}, bf16[1,256,512]{2,0,1:T(2,128)(2,1)}, u32[]{:S(2)}, u32[]{:S(2)}) %collective-permute-start.2) | collective-permute-done | bytes 262176 | tf_op jit(solution)/shard_map/ppermute | solution.py:19
  41.8 5.4 %collective-permute-done.3 = bf16[1,256,512]{2,0,1:T(2,128)(2,1)} collective-permute-done((bf16[1,256,512]{2,0,1:T(2,128)(2,1)S(1)}, bf16[1,256,512]{2,0,1:T(2,128)(2,1)}, u32[]{:S(2)}, u32[]{:S(2)}) %collective-permute-start.3) | collective-permute-done | bytes 262176 | tf_op jit(solution)/shard_map/ppermute | solution.py:22
  47.2 4.5 %convolution_convert_fusion.1 = bf16[4,256,512]{2,0,1:T(4,128)(2,1)S(1)} fusion(bf16[4,256,512]{2,0,1:T(4,128)(2,1)S(1)} %convolution_convert_fusion.2, bf16[1,256,512]{2,0,1:T(2,128)(2,1)} %collective-permute-done.3, bf16[1,256,512]{2,0,1:T(2,128)(2,1)} %collective-permute-done.2, bf16[1,256,512]{2,0,1:T(2,128)(2,1)} %collective-permute-done.1, ...), kind=kOutput, calls=%fused_computation.36 | convolution fusion | flops 11010064 | bytes 3145760 | tf_op jit(solution)/shard_map/ds,dnj->snj/dot_general | solution.py:68
  51.7 1.4 fusion.27
  54.5 1.7 fusion.59
  57.9 38.6 %all-gather.11.cloned.1.call-done = f32[2048,128]{1,0:T(8,128)} async-done(((f32[256,128]{1,0:T(8,128)}), f32[2048,128]{1,0:T(8,128)}) %all-gather.11.cloned.1.call-update) | async-done | bytes 1048592 | tf_op jit(solution)/shard_map/all_gather | solution.py:10
  96.5 1.9 reduce_sum.19
  98.8 14.5 %reshape_squeeze.6 = bf16[4,512,4,512]{3,2,1,0:T(4,128)(2,1)} reshape(bf16[1,1,2048,2048]{3,2,1,0:T(8,128)(2,1)} %param.18) | data formatting | bytes 16777216 | tf_op jit(solution)/shard_map/reshape;squeeze | solution.py:111
  113.4 6.6 %fusion.9 = f32[256,4,512,1]{2,0,3,1:T(8,128)S(1)} fusion(bf16[4,512,4,512]{3,2,1,0:T(4,128)(2,1)} %reshape_squeeze.6, bf16[4,256,512]{2,1,0:T(8,128)(2,1)} %copy-done.2, bf16[4,512]{1,0:T(4,128)(2,1)S(1)} %convert_element_type.89), kind=kOutput, calls=%fused_computation.11 | convolution fusion | flops 2149580800 | bytes 11538432 | tf_op jit(solution)/shard_map/gnj,gjfk->fnk/dot_general | solution.py:113
  120.0 19.6 %all-gather.7.cloned.1.call-done = bf16[256,2048]{1,0:T(8,128)(2,1)} async-done(((bf16[256,256]{1,0:T(8,128)(2,1)}), bf16[256,2048]{1,0:T(8,128)(2,1)}) %all-gather.7.cloned.1.call-update) | async-done | bytes 1048592 | tf_op jit(solution)/shard_map/all_gather | solution.py:131
  139.6 2.7 fusion.48
  142.2 54.2 %all-gather.9.cloned.1.call-done = f32[32,128,128]{2,1,0:T(8,128)} async-done(((f32[1,128,128]{2,1,0:T(8,128)}), f32[32,128,128]{2,1,0:T(8,128)}) %all-gather.9.cloned.1.call-update) | async-done | bytes 2097168 | tf_op jit(solution)/shard_map/all_gather | solution.py:29
  196.5 61.0 %all-gather.13.cloned.1.call-done = f32[8192,128]{1,0:T(8,128)} async-done(((f32[256,128]{1,0:T(8,128)}), f32[8192,128]{1,0:T(8,128)}) %all-gather.13.cloned.1.call-update) | async-done | bytes 4194320 | tf_op jit(solution)/shard_map/all_gather | solution.py:29
  257.4 71.3 %while.14 = (s32[]{:T(128)}, f32[256,128]{0,1:T(8,128)S(1)}, s32[]{:T(128)}, f32[32,128,128]{2,1,0:T(8,128)}, f32[32,256,128]{2,1,0:T(8,128)}, /*index=5*/s32[]{:T(128)}, s32[]{:T(128)}) while((s32[]{:T(128)}, f32[256,128]{0,1:T(8,128)S(1)}, s32[]{:T(128)}, f32[32,128,128]{2,1,0:T(8,128)}, f32[32,256,128]{2,1,0:T(8,128)}, ...), condition=%wide.region_3.4_spmd.clone, body=%wide.region_2.3_spmd.clone.sunk | while | flops 50462724 | bytes 1378403 | solution.py:41
  258.5 1.2 fusion.86
  260.7 1.2 fusion.86
  265.2 1.2 fusion.86
  278.5 1.2 fusion.86
  283.0 1.2 fusion.86
  287.4 1.2 fusion.86
  291.9 1.2 fusion.86
  296.4 1.2 fusion.86
  305.3 1.2 fusion.86
  309.7 1.2 fusion.86
  314.2 1.2 fusion.86
  318.6 1.2 fusion.86
  323.1 1.2 fusion.86
  328.7 1.3 fusion.33
  330.5 2.8 fusion.12
  333.3 3.3 multiply_convert_fusion
  336.7 1.6 fusion.70
  338.2 2.2 collective-permute-start.4
  340.4 6.4 %collective-permute-start.5 = (bf16[1,256,512]{2,0,1:T(2,128)(2,1)S(1)}, bf16[1,256,512]{2,0,1:T(2,128)(2,1)S(1)}, u32[]{:S(2)}, u32[]{:S(2)}) collective-permute-start(bf16[1,256,512]{2,0,1:T(2,128)(2,1)S(1)} %get-tuple-element.146), channel_id=1, source_target_pairs={{8,0},{16,8},{24,16},{32,24},{40,32},{48,40},{56,48},{64,56},{72,6... | collective-permute-start | bytes 786440 | tf_op jit(solution)/shard_map/ppermute | solution.py:22
  346.8 2.1 collective-permute-start.6
  349.0 3.7 collective-permute-start.7
  352.7 5.8 %collective-permute-done.4 = bf16[1,256,512]{2,0,1:T(2,128)(2,1)S(1)} collective-permute-done((bf16[1,256,512]{2,0,1:T(2,128)(2,1)S(1)}, bf16[1,256,512]{2,0,1:T(2,128)(2,1)S(1)}, u32[]{:S(2)}, u32[]{:S(2)}) %collective-permute-start.4) | collective-permute-done | bytes 262176 | tf_op jit(solution)/shard_map/ppermute | solution.py:19
  358.9 5.4 %collective-permute-done.6 = bf16[1,256,512]{2,0,1:T(2,128)(2,1)S(1)} collective-permute-done((bf16[1,256,512]{2,0,1:T(2,128)(2,1)S(1)}, bf16[1,256,512]{2,0,1:T(2,128)(2,1)S(1)}, u32[]{:S(2)}, u32[]{:S(2)}) %collective-permute-start.6) | collective-permute-done | bytes 262176 | tf_op jit(solution)/shard_map/ppermute | solution.py:19
  364.3 5.8 %collective-permute-done.7 = bf16[1,256,512]{2,0,1:T(2,128)(2,1)S(1)} collective-permute-done((bf16[1,256,512]{2,0,1:T(2,128)(2,1)S(1)}, bf16[1,256,512]{2,0,1:T(2,128)(2,1)S(1)}, u32[]{:S(2)}, u32[]{:S(2)}) %collective-permute-start.7) | collective-permute-done | bytes 262176 | tf_op jit(solution)/shard_map/ppermute | solution.py:22
  370.1 2.9 convolution_convert_fusion
  373.0 2.1 fusion.29
  (151 shorter events, 61.1 us)
Async XLA Ops:
  6.5 46.5 %copy-start = (bf16[1,1,2048,256]{3,2,1,0:T(8,128)(2,1)S(1)}, bf16[1,1,2048,256]{3,2,1,0:T(8,128)(2,1)}, u32[]{:S(2)}) copy-start(bf16[1,1,2048,256]{3,2,1,0:T(8,128)(2,1)} %param.19) | copy-start | bytes 3145732
  6.5 89.9 %all-gather.11.cloned.1.call-start = ((), (), s32[]{:S(2)}) async-start(), calls=%async_computation.2 | async-start | bytes 1179648 | tf_op jit(solution)/shard_map/all_gather | solution.py:10
  6.5 3.5 copy-start.4
  11.1 36.1 %copy-start.7 = (f32[1,1,4]{2,1,0:T(1,128)S(1)}, f32[1,1,4]{2,1,0:T(1,128)}, u32[]{:S(2)}) copy-start(f32[1,1,4]{2,1,0:T(1,128)} %param.16) | copy-start | bytes 52
  13.4 21.0 %collective-permute-start = (bf16[1,256,512]{2,0,1:T(2,128)(2,1)}, bf16[1,256,512]{2,0,1:T(2,128)(2,1)}, u32[]{:S(2)}, u32[]{:S(2)}) collective-permute-start(bf16[1,256,512]{2,0,1:T(2,128)(2,1)} %get-tuple-element.147), channel_id=1, source_target_pairs={{0,8},{8,16},{16,24},{24,32},{32,40},{40,48},{48,56},{56,64},{64,7... | collective-permute-start | bytes 786440 | tf_op jit(solution)/shard_map/ppermute | solution.py:19
  15.4 20.3 %collective-permute-start.1 = (bf16[1,256,512]{2,0,1:T(2,128)(2,1)}, bf16[1,256,512]{2,0,1:T(2,128)(2,1)}, u32[]{:S(2)}, u32[]{:S(2)}) collective-permute-start(bf16[1,256,512]{2,0,1:T(2,128)(2,1)} %get-tuple-element.150), channel_id=1, source_target_pairs={{8,0},{16,8},{24,16},{32,24},{40,32},{48,40},{56,48},{64,56},{72,6... | collective-permute-start | bytes 786440 | tf_op jit(solution)/shard_map/ppermute | solution.py:22
  23.0 18.8 %collective-permute-start.2 = (bf16[1,256,512]{2,0,1:T(2,128)(2,1)S(1)}, bf16[1,256,512]{2,0,1:T(2,128)(2,1)}, u32[]{:S(2)}, u32[]{:S(2)}) collective-permute-start(bf16[1,256,512]{2,0,1:T(2,128)(2,1)S(1)} %get-tuple-element.149), channel_id=1, source_target_pairs={{0,1},{1,2},{2,3},{3,4},{4,5},{5,6},{6,7},{8,9},{9,10},{10,11},{11... | collective-permute-start | bytes 786440 | tf_op jit(solution)/shard_map/ppermute | solution.py:19
  25.6 21.6 %collective-permute-start.3 = (bf16[1,256,512]{2,0,1:T(2,128)(2,1)S(1)}, bf16[1,256,512]{2,0,1:T(2,128)(2,1)}, u32[]{:S(2)}, u32[]{:S(2)}) collective-permute-start(bf16[1,256,512]{2,0,1:T(2,128)(2,1)S(1)} %get-tuple-element.148), channel_id=1, source_target_pairs={{1,0},{2,1},{3,2},{4,3},{5,4},{6,5},{7,6},{9,8},{10,9},{11,10},{12... | collective-permute-start | bytes 786440 | tf_op jit(solution)/shard_map/ppermute | solution.py:22
  47.2 4.5 %copy-start.3 = (s32[1,1,4,512]{3,2,1,0:T(4,128)S(1)}, s32[1,1,4,512]{3,2,1,0:T(4,128)}, u32[]{:S(2)}) copy-start(s32[1,1,4,512]{3,2,1,0:T(4,128)} %param.15) | copy-start | bytes 24580
  53.1 1.0 copy-start.2
  54.0 44.4 %copy-start.6 = (s32[1,1,256]{2,1,0:T(1,128)S(1)}, s32[1,1,256]{2,1,0:T(1,128)}, u32[]{:S(2)}) copy-start(s32[1,1,256]{2,1,0:T(1,128)} %param.17) | copy-start | bytes 3076
  54.5 1.8 copy-start.1
  56.2 83.3 %all-gather.7.cloned.1.call-start = ((), (), s32[]{:S(2)}) async-start(), calls=%async_computation | async-start | bytes 1179648 | tf_op jit(solution)/shard_map/all_gather | solution.py:131
  57.0 139.5 %all-gather.9.cloned.1.call-start = ((), (), s32[]{:S(2)}) async-start(), calls=%async_computation.1 | async-start | bytes 2162688 | tf_op jit(solution)/shard_map/all_gather | solution.py:29
  57.7 199.7 %all-gather.13.cloned.1.call-start = ((), (), s32[]{:S(2)}) async-start(), calls=%async_computation.3 | async-start | bytes 4325376 | tf_op jit(solution)/shard_map/all_gather | solution.py:29
  330.5 2.8 copy-start.5
  330.5 2.8 copy-start.8
  338.2 20.3 %collective-permute-start.4 = (bf16[1,256,512]{2,0,1:T(2,128)(2,1)S(1)}, bf16[1,256,512]{2,0,1:T(2,128)(2,1)S(1)}, u32[]{:S(2)}, u32[]{:S(2)}) collective-permute-start(bf16[1,256,512]{2,0,1:T(2,128)(2,1)S(1)} %get-tuple-element.143), channel_id=1, source_target_pairs={{0,8},{8,16},{16,24},{24,32},{32,40},{40,48},{48,56},{56,64},{64,7... | collective-permute-start | bytes 786440 | tf_op jit(solution)/shard_map/ppermute | solution.py:19
  340.4 18.5 %collective-permute-start.5 = (bf16[1,256,512]{2,0,1:T(2,128)(2,1)S(1)}, bf16[1,256,512]{2,0,1:T(2,128)(2,1)S(1)}, u32[]{:S(2)}, u32[]{:S(2)}) collective-permute-start(bf16[1,256,512]{2,0,1:T(2,128)(2,1)S(1)} %get-tuple-element.146), channel_id=1, source_target_pairs={{8,0},{16,8},{24,16},{32,24},{40,32},{48,40},{56,48},{64,56},{72,6... | collective-permute-start | bytes 786440 | tf_op jit(solution)/shard_map/ppermute | solution.py:22
  346.8 17.5 %collective-permute-start.6 = (bf16[1,256,512]{2,0,1:T(2,128)(2,1)S(1)}, bf16[1,256,512]{2,0,1:T(2,128)(2,1)S(1)}, u32[]{:S(2)}, u32[]{:S(2)}) collective-permute-start(bf16[1,256,512]{2,0,1:T(2,128)(2,1)S(1)} %get-tuple-element.145), channel_id=1, source_target_pairs={{0,1},{1,2},{2,3},{3,4},{4,5},{5,6},{6,7},{8,9},{9,10},{10,11},{11... | collective-permute-start | bytes 786440 | tf_op jit(solution)/shard_map/ppermute | solution.py:19
  349.0 21.1 %collective-permute-start.7 = (bf16[1,256,512]{2,0,1:T(2,128)(2,1)S(1)}, bf16[1,256,512]{2,0,1:T(2,128)(2,1)S(1)}, u32[]{:S(2)}, u32[]{:S(2)}) collective-permute-start(bf16[1,256,512]{2,0,1:T(2,128)(2,1)S(1)} %get-tuple-element.144), channel_id=1, source_target_pairs={{1,0},{2,1},{3,2},{4,3},{5,4},{6,5},{7,6},{9,8},{10,9},{11,10},{12... | collective-permute-start | bytes 786440 | tf_op jit(solution)/shard_map/ppermute | solution.py:22
Sparse Core Ops, SparseCore 0:
  56.3 40.1 all-gather.10
  98.2 41.3 all-gather.6
  142.1 54.2 all-gather.8
  198.9 58.5 all-gather.12
